TPU v7x, 32 devices: a whole 2x2x4 slice. The times are simulated.
32 devices in a mesh: rep: 4 (over z), fsdp: 2 (over x), seq: 4 (over y, core).
Axes of the slice: x: 2, y: 2, z: 4, core: 2. Of those that a mesh axis runs over, the one named last changes fastest.
Arguments:
- tokens: bfloat16 [8, 1024, 640], P(('rep', 'fsdp'), 'seq'), may hold values from -6 to 6
- d_out: bfloat16 [8, 1024, 640], P(('rep', 'fsdp'), 'seq'), may hold values from -6 to 6
- doc_lengths: int32 [8, 3], P(('rep', 'fsdp')), may hold values from 1 to 640, 1024 in all within a row
- w_query: bfloat16 [640, 1024], P('fsdp'), may hold values from -0.25 to 0.25
- w_key: bfloat16 [640, 256], P('fsdp'), may hold values from -0.25 to 0.25
- w_value: bfloat16 [640, 256], P('fsdp'), may hold values from -0.25 to 0.25
- w_out: bfloat16 [1024, 640], P('fsdp'), may hold values from -0.1875 to 0.1875
- w_gate: bfloat16 [640, 2048], P('fsdp'), may hold values from -0.25 to 0.25
- w_up: bfloat16 [640, 2048], P('fsdp'), may hold values from -0.25 to 0.25
- w_down: bfloat16 [2048, 640], P('fsdp'), may hold values from -0.125 to 0.125
- g_input: bfloat16 [640], P('fsdp'), may hold values from 0.5 to 1.5
- g_query: bfloat16 [256], P('fsdp'), may hold values from 0.25 to 1.75
- g_key: bfloat16 [256], P('fsdp'), may hold values from 0.25 to 1.75
- g_attn: bfloat16 [640], P('fsdp'), may hold values from 0.5 to 1.5
- g_ffin: bfloat16 [640], P('fsdp'), may hold values from 0.5 to 1.5
- g_ffout: bfloat16 [640], P('fsdp'), may hold values from 0.5 to 1.5
Outputs:
- result: bfloat16 [8, 1024, 640], P(('rep', 'fsdp'), 'seq')
- d_tokens: bfloat16 [8, 1024, 640], P(('rep', 'fsdp'), 'seq')
- grad_query: float32 [640, 1024], P('fsdp')
- grad_key: float32 [640, 256], P('fsdp')
- grad_value: float32 [640, 256], P('fsdp')
- grad_out: float32 [1024, 640], P('fsdp')
- grad_gate: float32 [640, 2048], P('fsdp')
- grad_up: float32 [640, 2048], P('fsdp')
- grad_down: float32 [2048, 640], P('fsdp')
- grad_ginput: float32 [640], P('fsdp')
- grad_gquery: float32 [256], P('fsdp')
- grad_gkey: float32 [256], P('fsdp')
- grad_gattn: float32 [640], P('fsdp')
- grad_gffin: float32 [640], P('fsdp')
- grad_gffout: float32 [640], P('fsdp')
Inputs may be any that keep to these rules, and one draw needn't show every extreme that they name: `doc_lengths`: each row lists the lengths of the 3 documents packed in order into one sequence; a row sums to 1024 and its largest entry is 640.
All inputs are finite; a program needn't handle non-finite values.
Results may differ from a plain program's by a relative error of at most 0.024.
Values may be sent and summed in bfloat16 or wider, within the bound.
A program may use at most 128 MiB of HBM per device.

v0:
```python
import jax
import jax.numpy as jnp
from jax import lax
from jax.sharding import PartitionSpec as P

EPS = 1e-06
ROPE_BASE = 1000000.0
MASKED = -1e30


def rms_norm(values, gain_vec):
    return values * lax.rsqrt(jnp.mean(values * values, axis=-1, keepdims=True) + EPS) * gain_vec


def rotate(values, angles):
    half_width = values.shape[-1] // 2
    front_half = values[..., :half_width]
    back_half = values[..., half_width:]
    cos_part = jnp.cos(angles)
    sin_part = jnp.sin(angles)
    return jnp.concatenate(
        [
            front_half * cos_part - back_half * sin_part,
            back_half * cos_part + front_half * sin_part,
        ],
        axis=-1,
    )


def frequencies(head_size):
    return jnp.power(
        jnp.float32(ROPE_BASE), -2.0 * jnp.arange(head_size // 2, dtype=jnp.float32) / head_size
    )


def layout(lengths_row, total_len):
    doc_ends = jnp.cumsum(lengths_row)
    starts = doc_ends - lengths_row
    indices = jnp.arange(total_len, dtype=jnp.int32)
    segment = jnp.sum((indices[:, None] >= doc_ends[None, :]).astype(jnp.int32), axis=1)
    onehot = segment[:, None] == jnp.arange(lengths_row.shape[0], dtype=jnp.int32)[None, :]
    doc_begin = jnp.sum(jnp.where(onehot, starts[None, :], 0), axis=1)
    return (segment, indices - doc_begin)


def matmul(left_side, right_side):
    return jnp.dot(left_side, right_side, preferred_element_type=jnp.float32)


def times_transpose(left_side, right_side):
    return lax.dot_general(
        left_side, right_side, (((1,), (1,)), ((), ())), preferred_element_type=jnp.float32
    )


def transpose_times(left_side, right_side):
    return lax.dot_general(
        left_side, right_side, (((0,), (0,)), ((), ())), preferred_element_type=jnp.float32
    )


def gated(gate_proj, up_proj):
    return jax.nn.gelu(gate_proj, approximate=True) * up_proj


def body(
    tokens,
    d_out,
    doc_lengths,
    w_query,
    w_key,
    w_value,
    w_out,
    w_gate,
    w_up,
    w_down,
    g_input,
    g_query,
    g_key,
    g_attn,
    g_ffin,
    g_ffout,
):
    gathered = (
        lax.all_gather(w_query, "fsdp", axis=0, tiled=True),
        lax.all_gather(w_key, "fsdp", axis=0, tiled=True),
        lax.all_gather(w_value, "fsdp", axis=0, tiled=True),
        lax.all_gather(w_out, "fsdp", axis=0, tiled=True),
        lax.all_gather(w_gate, "fsdp", axis=0, tiled=True),
        lax.all_gather(w_up, "fsdp", axis=0, tiled=True),
        lax.all_gather(w_down, "fsdp", axis=0, tiled=True),
        lax.all_gather(g_input, "fsdp", axis=0, tiled=True),
        lax.all_gather(g_query, "fsdp", axis=0, tiled=True),
        lax.all_gather(g_key, "fsdp", axis=0, tiled=True),
        lax.all_gather(g_attn, "fsdp", axis=0, tiled=True),
        lax.all_gather(g_ffin, "fsdp", axis=0, tiled=True),
        lax.all_gather(g_ffout, "fsdp", axis=0, tiled=True),
    )
    query_mat, key_mat, value_mat, out_mat, gate_mat, up_mat, down_mat = gathered[:7]
    gain_input, gain_query, gain_key, gain_attn, gain_ffin, gain_ffout = [
        entry.astype(jnp.float32) for entry in gathered[7:]
    ]
    row_count = tokens.shape[1]
    head_size = gain_query.shape[0]
    head_count = query_mat.shape[1] // head_size
    total_len = row_count * lax.axis_size("seq")
    segment, position = layout(doc_lengths[0], total_len)
    offset = lax.axis_index("seq") * row_count
    query_seg = lax.dynamic_slice_in_dim(segment, offset, row_count)
    query_pos = lax.dynamic_slice_in_dim(position, offset, row_count)
    places = offset + jnp.arange(row_count, dtype=jnp.int32)
    allowed = (query_seg[:, None] == segment[None, :]) & (
        places[:, None] >= jnp.arange(total_len, dtype=jnp.int32)[None, :]
    )
    angles = query_pos.astype(jnp.float32)[:, None] * frequencies(head_size)[None, :]
    scaling = head_size ** (-0.5)
    inputs = tokens[0].astype(jnp.float32)
    cotangent = d_out[0].astype(jnp.float32)
    input_norm, input_pull = jax.vjp(rms_norm, inputs, gain_input)
    attn_input = input_norm.astype(jnp.bfloat16)
    q_proj = matmul(attn_input, query_mat)
    k_proj = matmul(attn_input, key_mat)
    v_proj = matmul(attn_input, value_mat)

    def query_fn(projected, gain_vec):
        shaped = projected.reshape(projected.shape[0], -1, gain_vec.shape[0])
        return rotate(rms_norm(shaped, gain_vec), angles[:, None, :])

    def key_fn(projected, gain_vec):
        return rotate(rms_norm(projected, gain_vec), angles)

    queries, query_pull = jax.vjp(query_fn, q_proj, gain_query)
    keys_own, key_pull = jax.vjp(key_fn, k_proj, gain_key)
    query_rows = queries.astype(jnp.bfloat16).reshape(row_count * head_count, head_size)
    key_rows, value_rows = (
        lax.all_gather(keys_own.astype(jnp.bfloat16), "seq", axis=0, tiled=True),
        lax.all_gather(v_proj.astype(jnp.bfloat16), "seq", axis=0, tiled=True),
    )

    def masked_scores():
        raw_scores = times_transpose(query_rows, key_rows).reshape(row_count, head_count, total_len)
        return jnp.where(allowed[:, None, :], raw_scores * scaling, MASKED)

    scores = masked_scores()
    top_score = jnp.max(scores, axis=-1, keepdims=True)
    shifted = jnp.exp(scores - top_score)
    denominator = jnp.sum(shifted, axis=-1, keepdims=True)
    log_total = top_score + jnp.log(denominator)
    probs_low = (
        (shifted / denominator).astype(jnp.bfloat16).reshape(row_count * head_count, total_len)
    )
    mixed_rows = (
        matmul(probs_low, value_rows)
        .reshape(row_count, head_count * head_size)
        .astype(jnp.bfloat16)
    )
    out_proj = matmul(mixed_rows, out_mat)
    attn_norm, attn_pull = jax.vjp(rms_norm, out_proj, gain_attn)
    hidden_one = inputs + attn_norm
    ffin_norm, ffin_pull = jax.vjp(rms_norm, hidden_one, gain_ffin)
    ff_input = ffin_norm.astype(jnp.bfloat16)
    gate_proj = matmul(ff_input, gate_mat)
    up_proj = matmul(ff_input, up_mat)
    activated, gated_pull = jax.vjp(gated, gate_proj, up_proj)
    hidden = activated.astype(jnp.bfloat16)
    down_proj = matmul(hidden, down_mat)
    ffout_norm, ffout_pull = jax.vjp(rms_norm, down_proj, gain_ffout)
    result = hidden_one + ffout_norm
    query_mat, key_mat, value_mat, out_mat, gate_mat, up_mat, down_mat = (
        lax.all_gather(w_query, "fsdp", axis=0, tiled=True),
        lax.all_gather(w_key, "fsdp", axis=0, tiled=True),
        lax.all_gather(w_value, "fsdp", axis=0, tiled=True),
        lax.all_gather(w_out, "fsdp", axis=0, tiled=True),
        lax.all_gather(w_gate, "fsdp", axis=0, tiled=True),
        lax.all_gather(w_up, "fsdp", axis=0, tiled=True),
        lax.all_gather(w_down, "fsdp", axis=0, tiled=True),
    )
    d_down, grad_gffout = ffout_pull(cotangent)
    d_down_low = d_down.astype(jnp.bfloat16)
    grad_down = transpose_times(hidden, d_down_low)
    d_hidden = times_transpose(d_down_low, down_mat)
    d_gate, d_up = gated_pull(d_hidden)
    d_gate_low = d_gate.astype(jnp.bfloat16)
    d_up_low = d_up.astype(jnp.bfloat16)
    grad_gate = transpose_times(ff_input, d_gate_low)
    grad_up = transpose_times(ff_input, d_up_low)
    d_ffin = times_transpose(d_gate_low, gate_mat) + times_transpose(d_up_low, up_mat)
    d_hidden_part, grad_gffin = ffin_pull(d_ffin)
    d_hidden_one = cotangent + d_hidden_part
    d_out_proj, grad_gattn = attn_pull(d_hidden_one)
    d_out_low = d_out_proj.astype(jnp.bfloat16)
    grad_out = transpose_times(mixed_rows, d_out_low)
    d_mixed = (
        times_transpose(d_out_low, out_mat)
        .astype(jnp.bfloat16)
        .reshape(row_count * head_count, head_size)
    )
    probs_full = jnp.exp(masked_scores() - log_total)
    d_probs = times_transpose(d_mixed, value_rows).reshape(row_count, head_count, total_len)
    row_dot = jnp.sum(probs_full * d_probs, axis=-1, keepdims=True)
    d_raw = (
        (probs_full * (d_probs - row_dot) * scaling)
        .astype(jnp.bfloat16)
        .reshape(row_count * head_count, total_len)
    )
    d_queries = matmul(d_raw, key_rows).reshape(row_count, head_count, head_size)
    grad_key_rows = transpose_times(d_raw, query_rows)
    grad_value_rows = transpose_times(probs_low, d_mixed)
    d_keys_own, d_values_own = (
        lax.psum_scatter(
            grad_key_rows.astype(jnp.bfloat16), "seq", scatter_dimension=0, tiled=True
        ).astype(jnp.float32),
        lax.psum_scatter(
            grad_value_rows.astype(jnp.bfloat16), "seq", scatter_dimension=0, tiled=True
        ).astype(jnp.float32),
    )
    d_q_proj, grad_gquery = query_pull(d_queries)
    d_k_proj, grad_gkey = key_pull(d_keys_own)
    d_q_low = d_q_proj.astype(jnp.bfloat16)
    d_k_low = d_k_proj.astype(jnp.bfloat16)
    d_v_low = d_values_own.astype(jnp.bfloat16)
    grad_query = transpose_times(attn_input, d_q_low)
    grad_key = transpose_times(attn_input, d_k_low)
    grad_value = transpose_times(attn_input, d_v_low)
    d_attn_input = (
        times_transpose(d_q_low, query_mat)
        + times_transpose(d_k_low, key_mat)
        + times_transpose(d_v_low, value_mat)
    )
    d_inputs_part, grad_ginput = input_pull(d_attn_input)
    d_inputs = d_hidden_one + d_inputs_part
    shards = (
        lax.psum_scatter(
            grad_query.astype(jnp.bfloat16), "fsdp", scatter_dimension=0, tiled=True
        ).astype(jnp.float32),
        lax.psum_scatter(
            grad_key.astype(jnp.bfloat16), "fsdp", scatter_dimension=0, tiled=True
        ).astype(jnp.float32),
        lax.psum_scatter(
            grad_value.astype(jnp.bfloat16), "fsdp", scatter_dimension=0, tiled=True
        ).astype(jnp.float32),
        lax.psum_scatter(
            grad_out.astype(jnp.bfloat16), "fsdp", scatter_dimension=0, tiled=True
        ).astype(jnp.float32),
        lax.psum_scatter(
            grad_gate.astype(jnp.bfloat16), "fsdp", scatter_dimension=0, tiled=True
        ).astype(jnp.float32),
        lax.psum_scatter(
            grad_up.astype(jnp.bfloat16), "fsdp", scatter_dimension=0, tiled=True
        ).astype(jnp.float32),
        lax.psum_scatter(
            grad_down.astype(jnp.bfloat16), "fsdp", scatter_dimension=0, tiled=True
        ).astype(jnp.float32),
        lax.psum_scatter(
            grad_ginput.astype(jnp.bfloat16), "fsdp", scatter_dimension=0, tiled=True
        ).astype(jnp.float32),
        lax.psum_scatter(
            grad_gquery.astype(jnp.bfloat16), "fsdp", scatter_dimension=0, tiled=True
        ).astype(jnp.float32),
        lax.psum_scatter(
            grad_gkey.astype(jnp.bfloat16), "fsdp", scatter_dimension=0, tiled=True
        ).astype(jnp.float32),
        lax.psum_scatter(
            grad_gattn.astype(jnp.bfloat16), "fsdp", scatter_dimension=0, tiled=True
        ).astype(jnp.float32),
        lax.psum_scatter(
            grad_gffin.astype(jnp.bfloat16), "fsdp", scatter_dimension=0, tiled=True
        ).astype(jnp.float32),
        lax.psum_scatter(
            grad_gffout.astype(jnp.bfloat16), "fsdp", scatter_dimension=0, tiled=True
        ).astype(jnp.float32),
    )
    totals = (
        lax.psum(shards[0].astype(jnp.bfloat16), ("rep", "seq")).astype(jnp.float32),
        lax.psum(shards[1].astype(jnp.bfloat16), ("rep", "seq")).astype(jnp.float32),
        lax.psum(shards[2].astype(jnp.bfloat16), ("rep", "seq")).astype(jnp.float32),
        lax.psum(shards[3].astype(jnp.bfloat16), ("rep", "seq")).astype(jnp.float32),
        lax.psum(shards[4].astype(jnp.bfloat16), ("rep", "seq")).astype(jnp.float32),
        lax.psum(shards[5].astype(jnp.bfloat16), ("rep", "seq")).astype(jnp.float32),
        lax.psum(shards[6].astype(jnp.bfloat16), ("rep", "seq")).astype(jnp.float32),
        lax.psum(shards[7].astype(jnp.bfloat16), ("rep", "seq")).astype(jnp.float32),
        lax.psum(shards[8].astype(jnp.bfloat16), ("rep", "seq")).astype(jnp.float32),
        lax.psum(shards[9].astype(jnp.bfloat16), ("rep", "seq")).astype(jnp.float32),
        lax.psum(shards[10].astype(jnp.bfloat16), ("rep", "seq")).astype(jnp.float32),
        lax.psum(shards[11].astype(jnp.bfloat16), ("rep", "seq")).astype(jnp.float32),
        lax.psum(shards[12].astype(jnp.bfloat16), ("rep", "seq")).astype(jnp.float32),
    )
    return (
        result.astype(jnp.bfloat16)[None],
        d_inputs.astype(jnp.bfloat16)[None],
        totals[0],
        totals[1],
        totals[2],
        totals[3],
        totals[4],
        totals[5],
        totals[6],
        totals[7],
        totals[8],
        totals[9],
        totals[10],
        totals[11],
        totals[12],
    )


def solution(mesh):
    in_specs = (
        P(("rep", "fsdp"), "seq", None),
        P(("rep", "fsdp"), "seq", None),
        P(("rep", "fsdp"), None),
        P("fsdp", None),
        P("fsdp", None),
        P("fsdp", None),
        P("fsdp", None),
        P("fsdp", None),
        P("fsdp", None),
        P("fsdp", None),
        P("fsdp"),
        P("fsdp"),
        P("fsdp"),
        P("fsdp"),
        P("fsdp"),
        P("fsdp"),
    )
    out_specs = (
        P(("rep", "fsdp"), "seq", None),
        P(("rep", "fsdp"), "seq", None),
        P("fsdp", None),
        P("fsdp", None),
        P("fsdp", None),
        P("fsdp", None),
        P("fsdp", None),
        P("fsdp", None),
        P("fsdp", None),
        P("fsdp"),
        P("fsdp"),
        P("fsdp"),
        P("fsdp"),
        P("fsdp"),
        P("fsdp"),
    )
    return jax.shard_map(body, mesh=mesh, in_specs=in_specs, out_specs=out_specs, check_vma=False)
```

profile of v0, /device:TPU:0, one launch (start us, length us, event | category | flops | bytes accessed | tf_op | source)
XLA Modules:
  0.0 610.9 jit_solution(18083511794878233762)
XLA Ops:
  11.2 5.2 all-gather
  16.3 4.2 all-gather.1
  22.8 5.3 all-reduce.17
  29.0 10.0 %all_gather.55 = bf16[640,256]{1,0:T(8,128)(2,1)S(1)} all-gather(bf16[320,256]{1,0:T(8,128)(2,1)S(1)} %copy-done.38), channel_id=1, replica_groups=mesh['rep'=4,'fsdp'=2,'seq'=4] {'fsdp'}, dimensions={0}, use_global_device_ids=true | all-gather | bytes 491520 | tf_op jit(solution)/shard_map/all_gather | solution.py:86
  39.5 6.0 all_gather.58
  45.8 8.1 %all_gather.59 = bf16[1024,256]{1,0:T(8,128)(2,1)} all-gather(bf16[256,256]{1,0:T(8,128)(2,1)S(1)} %convolution_convert_fusion.10), channel_id=1, replica_groups=mesh['rep'=4,'fsdp'=2,'seq'=4] {'seq'}, dimensions={0}, use_global_device_ids=true | all-gather | bytes 655360 | tf_op jit(solution)/shard_map/all_gather | solution.py:137
  54.7 7.3 %all_gather.57 = bf16[1024,256]{0,1:T(8,128)(2,1)S(1)} all-gather(bf16[256,256]{0,1:T(8,128)(2,1)S(1)} %pad_maximum_fusion.3), channel_id=1, replica_groups=mesh['rep'=4,'fsdp'=2,'seq'=4] {'seq'}, dimensions={0}, use_global_device_ids=true | all-gather | bytes 655360 | tf_op jit(solution)/shard_map/all_gather | solution.py:136
  80.6 26.2 %all-gather.12.cloned.1.call-done = bf16[640,2048]{1,0:T(8,128)(2,1)} async-done(((bf16[320,2048]{1,0:T(8,128)(2,1)}), bf16[640,2048]{1,0:T(8,128)(2,1)}) %all-gather.12.cloned.1.call-update) | async-done | bytes 2621456 | tf_op jit(solution)/shard_map/all_gather | solution.py:89
  106.9 4.0 fusion.103
  110.9 36.4 %all-gather.14.cloned.1.call-done = bf16[640,2048]{1,0:T(8,128)(2,1)} async-done(((bf16[320,2048]{1,0:T(8,128)(2,1)}), bf16[640,2048]{1,0:T(8,128)(2,1)}) %all-gather.14.cloned.1.call-update) | async-done | bytes 2621456 | tf_op jit(solution)/shard_map/all_gather | solution.py:90
  147.3 5.2 multiply_convert_fusion.2
  152.6 35.2 %all-gather.16.cloned.1.call-done = bf16[2048,640]{1,0:T(8,128)(2,1)} async-done(((bf16[1024,640]{1,0:T(8,128)(2,1)}), bf16[2048,640]{1,0:T(8,128)(2,1)}) %all-gather.16.cloned.1.call-update) | async-done | bytes 2621456 | tf_op jit(solution)/shard_map/all_gather | solution.py:91
  210.5 12.4 %fusion.27 = bf16[1024,256]{0,1:T(8,128)(2,1)} fusion(f32[256,4,1024]{2,0,1:T(8,128)} %fusion.54, f32[256,4,1024]{2,0,1:T(8,128)} %copy-done, f32[256,4]{0,1:T(4,128)S(1)} %log_add_fusion, bf16[256,4,128]{0,2,1:T(8,128)(2,1)} %copy-done.36, bf16[256,4,128]{0,2,1:T(8,128)(2,1)S(1)} %copy-done.35), kind=kOutput, calls=%fused_computation.34 | convolution fusion | flops 545523712 | bytes 9441280 | tf_op jit(solution)/shard_map/dot_general | solution.py:57
  223.0 5.3 reduce-scatter.12.cloned.1.call-done
  230.5 22.6 %reduce-scatter.10.cloned.1.call-done = bf16[256,256]{0,1:T(8,128)(2,1)} async-done(((bf16[1024,256]{0,1:T(8,128)(2,1)}), bf16[256,256]{0,1:T(8,128)(2,1)}) %reduce-scatter.10.cloned.1.call-update) | async-done | bytes 131088 | tf_op jit(solution)/shard_map/reduce_scatter | solution.py:210
  257.9 10.5 %fusion.9 = f32[256,4,256]{0,2,1:T(8,128)S(1)} fusion(f32[256,4,1024]{2,0,1:T(8,128)} %fusion.54, f32[256,4,1024]{2,0,1:T(8,128)} %copy-done, f32[256,4]{0,1:T(4,128)S(1)} %log_add_fusion, bf16[1024,256]{0,1:T(8,128)(2,1)} %copy-done.33), kind=kOutput, calls=%fused_computation.15 | convolution fusion | flops 544212992 | bytes 9965568 | tf_op jit(solution)/shard_map/dot_general | solution.py:47
  283.2 26.0 %reduce-scatter.20.cloned.1.call-done = bf16[512,640]{1,0:T(8,128)(2,1)} async-done(((bf16[1024,640]{1,0:T(8,128)(2,1)}), bf16[512,640]{1,0:T(8,128)(2,1)}) %reduce-scatter.20.cloned.1.call-update) | async-done | bytes 655376 | tf_op jit(solution)/shard_map/reduce_scatter | solution.py:242
  309.2 26.1 %reduce-scatter.14.cloned.1.call-done = bf16[320,1024]{1,0:T(8,128)(2,1)} async-done(((bf16[640,1024]{1,0:T(8,128)(2,1)}), bf16[320,1024]{1,0:T(8,128)(2,1)}) %reduce-scatter.14.cloned.1.call-update) | async-done | bytes 655376 | tf_op jit(solution)/shard_map/reduce_scatter | solution.py:233
  335.3 40.4 %reduce-scatter.24.cloned.1.call-done = bf16[320,2048]{1,0:T(8,128)(2,1)} async-done(((bf16[640,2048]{1,0:T(8,128)(2,1)}), bf16[320,2048]{1,0:T(8,128)(2,1)}) %reduce-scatter.24.cloned.1.call-update) | async-done | bytes 1310736 | tf_op jit(solution)/shard_map/reduce_scatter | solution.py:248
  375.7 40.5 %reduce-scatter.22.cloned.1.call-done = bf16[320,2048]{1,0:T(8,128)(2,1)} async-done(((bf16[640,2048]{1,0:T(8,128)(2,1)}), bf16[320,2048]{1,0:T(8,128)(2,1)}) %reduce-scatter.22.cloned.1.call-update) | async-done | bytes 1310736 | tf_op jit(solution)/shard_map/reduce_scatter | solution.py:245
  416.2 40.4 %reduce-scatter.26.cloned.1.call-done = bf16[1024,640]{1,0:T(8,128)(2,1)} async-done(((bf16[2048,640]{1,0:T(8,128)(2,1)}), bf16[1024,640]{1,0:T(8,128)(2,1)}) %reduce-scatter.26.cloned.1.call-update) | async-done | bytes 1310736 | tf_op jit(solution)/shard_map/reduce_scatter | solution.py:251
  459.6 5.1 all-reduce.16
  465.1 34.6 %all-reduce.14 = (bf16[320]{0:T(512)(128)(2,1)S(1)}, bf16[128]{0:T(256)(128)(2,1)S(1)}, bf16[128]{0:T(256)(128)(2,1)S(1)}, bf16[320]{0:T(512)(128)(2,1)S(1)}, bf...) all-reduce(bf16[320]{0:T(512)(128)(2,1)S(1)} %dynamic-slice.5, ...), channel_id=1, replica_groups=mesh['rep'=4,'fsdp'=2,'seq'=4] {'rep','seq'}, use_global_device_ids=true, to_apply=%region_36.37 | all-reduce | flops 1536 | bytes 6144 | tf_op jit(solution)/shard_map/psum | solution.py:281
  504.0 88.2 %all-reduce.20.cloned.1.call-done = (bf16[320,1024]{1,0:T(8,128)(2,1)}, bf16[320,256]{1,0:T(8,128)(2,1)}, bf16[320,256]{1,0:T(8,128)(2,1)}, bf16[512,640]{1,0:T(...) async-done(((bf16[320,1024]{1,0:T(8,128)(2,1)}, bf16[320,256]{1,0:T(8,128)(2,1)}, bf16[320,256]{1,0:T(8,128)(2,1)}, ...) | async-done | bytes 5570576 | tf_op jit(solution)/shard_map/psum | solution.py:274
  (313 shorter events, 88.5 us)
Async XLA Ops:
  7.2 55.9 %all-gather.8.cloned.1.call-start = ((), (), s32[]{:S(2)}) async-start(), calls=%async_computation.9 | async-start | bytes 1966080 | tf_op jit(solution)/shard_map/all_gather | solution.py:85
  7.9 69.0 %all-gather.10.cloned.1.call-start = ((), (), s32[]{:S(2)}) async-start(), calls=%async_computation.10 | async-start | bytes 1966080 | tf_op jit(solution)/shard_map/all_gather | solution.py:88
  8.8 98.1 %all-gather.12.cloned.1.call-start = ((), (), s32[]{:S(2)}) async-start(), calls=%async_computation.11 | async-start | bytes 3932160 | tf_op jit(solution)/shard_map/all_gather | solution.py:89
  9.5 137.8 %all-gather.14.cloned.1.call-start = ((), (), s32[]{:S(2)}) async-start(), calls=%async_computation.12 | async-start | bytes 3932160 | tf_op jit(solution)/shard_map/all_gather | solution.py:90
  10.1 177.6 %all-gather.16.cloned.1.call-start = ((), (), s32[]{:S(2)}) async-start(), calls=%async_computation.13 | async-start | bytes 3932160 | tf_op jit(solution)/shard_map/all_gather | solution.py:91
  10.7 217.7 %reduce-scatter.12.cloned.1.call-start = ((), (), s32[]{:S(2)}) async-start(), calls=%async_computation.15 | async-start | bytes 655360 | tf_op jit(solution)/shard_map/reduce_scatter | solution.py:213
  10.8 43.3 %copy-start.75 = (f32[128]{0:T(128)}, f32[128]{0:T(128)S(1)}, u32[]{:S(2)}) copy-start(f32[128]{0:T(128)S(1)} %multiply_power_fusion) | copy-start | bytes 1540
  11.1 42.9 %copy-start.62 = (f32[256]{0:T(256)}, f32[256]{0:T(256)S(1)}, u32[]{:S(2)}) copy-start(f32[256]{0:T(256)S(1)} %fusion.45) | copy-start | bytes 3076
  11.1 53.7 %copy-start.48 = (f32[256]{0:T(256)}, f32[256]{0:T(256)S(1)}, u32[]{:S(2)}) copy-start(f32[256]{0:T(256)S(1)} %fusion.83) | copy-start | bytes 3076
  16.3 49.2 %copy-start.52 = (f32[2,1,128]{2,1,0:T(1,128)}, f32[2,1,128]{2,1,0:T(1,128)S(1)}, u32[]{:S(2)}) copy-start(f32[2,1,128]{2,1,0:T(1,128)S(1)} %convert_element_type.284) | copy-start | bytes 3076
  20.6 33.5 %copy-start.54 = (f32[2,1,128]{2,1,0:T(1,128)}, f32[2,1,128]{2,1,0:T(1,128)S(1)}, u32[]{:S(2)}) copy-start(f32[2,1,128]{2,1,0:T(1,128)S(1)} %convert_element_type.285) | copy-start | bytes 3076
  206.5 46.6 %reduce-scatter.10.cloned.1.call-start = ((), (), s32[]{:S(2)}) async-start(), calls=%async_computation.14 | async-start | bytes 655360 | tf_op jit(solution)/shard_map/reduce_scatter | solution.py:210
  222.9 31.7 %copy-start.57 = (f32[256]{0:T(256)S(1)}, f32[256]{0:T(256)}, u32[]{:S(2)}) copy-start(f32[256]{0:T(256)} %copy-done.56) | copy-start | bytes 3076
  222.9 31.9 %copy-start.72 = (f32[256]{0:T(256)S(1)}, f32[256]{0:T(256)}, u32[]{:S(2)}) copy-start(f32[256]{0:T(256)} %copy-done.71) | copy-start | bytes 3076
  223.0 58.9 %reduce-scatter.18.cloned.1.call-start = ((), (), s32[]{:S(2)}) async-start(), calls=%async_computation.18 | async-start | bytes 491520 | tf_op jit(solution)/shard_map/reduce_scatter | solution.py:239
  230.4 52.8 %reduce-scatter.16.cloned.1.call-start = ((), (), s32[]{:S(2)}) async-start(), calls=%async_computation.17 | async-start | bytes 491520 | tf_op jit(solution)/shard_map/reduce_scatter | solution.py:236
  256.1 53.0 %reduce-scatter.20.cloned.1.call-start = ((), (), s32[]{:S(2)}) async-start(), calls=%async_computation.19 | async-start | bytes 1966080 | tf_op jit(solution)/shard_map/reduce_scatter | solution.py:242
  257.9 77.4 %reduce-scatter.14.cloned.1.call-start = ((), (), s32[]{:S(2)}) async-start(), calls=%async_computation.16 | async-start | bytes 1966080 | tf_op jit(solution)/shard_map/reduce_scatter | solution.py:233
  271.9 103.7 %reduce-scatter.24.cloned.1.call-start = ((), (), s32[]{:S(2)}) async-start(), calls=%async_computation.21 | async-start | bytes 3932160 | tf_op jit(solution)/shard_map/reduce_scatter | solution.py:248
  274.4 141.8 %reduce-scatter.22.cloned.1.call-start = ((), (), s32[]{:S(2)}) async-start(), calls=%async_computation.20 | async-start | bytes 3932160 | tf_op jit(solution)/shard_map/reduce_scatter | solution.py:245
  278.0 178.6 %reduce-scatter.26.cloned.1.call-start = ((), (), s32[]{:S(2)}) async-start(), calls=%async_computation.22 | async-start | bytes 3932160 | tf_op jit(solution)/shard_map/reduce_scatter | solution.py:251
  281.8 310.4 %all-reduce.20.cloned.1.call-start = ((), (), s32[]{:S(2)}) async-start(), calls=%async_computation.23 | async-start | bytes 11141120 | tf_op jit(solution)/shard_map/psum | solution.py:274
  458.8 44.3 %copy-start.63 = (f32[256]{0:T(256)S(1)}, f32[256]{0:T(256)}, u32[]{:S(2)}) copy-start(f32[256]{0:T(256)} %copy-done.62) | copy-start | bytes 3076
  458.8 44.3 %copy-start.3 = (f32[256,640]{1,0:T(8,128)S(1)}, f32[256,640]{1,0:T(8,128)}, u32[]{:S(2)}) copy-start(f32[256,640]{1,0:T(8,128)} %copy-done.2) | copy-start | bytes 1966084
  (77 other events, 539.1 us)
Sparse Core Ops, SparseCore 0:
  9.5 31.1 all-gather.7
  42.2 24.0 all-gather.9
  67.8 38.9 all-gather.11
  108.3 38.9 all-gather.13
  148.7 38.9 all-gather.15
  206.7 21.6 reduce-scatter.11
  231.4 21.6 reduce-scatter.9
  255.3 12.4 reduce-scatter.17
  270.7 12.4 reduce-scatter.15
  285.8 23.2 reduce-scatter.19
  312.0 23.2 reduce-scatter.13
  338.0 37.6 reduce-scatter.23
  378.5 37.6 reduce-scatter.21
  418.9 37.6 reduce-scatter.25
  461.1 131.0 all-reduce.19
where the time goes:
time: 612 us; the launch traced here: 611 us
  waiting for transfers between devices  392 us (64%)
  blocking collectives  85.7 us (14%)
  matrix products  70.8 us (12%)
  other arithmetic  28 us (5%)
  between operations  17.2 us (3%)
  local copies, waits for them, and re-layouts  16.7 us (3%)
    psum x1, waiting for transfers between devices, body(): lax.psum(shards[0].astype(jnp.bfloat16), ('rep', 'seq')).astype(jnp.float32)  88.2 us
    reduce_scatter x1, waiting for transfers between devices, body(): lax.psum_scatter(grad_gate.astype(jnp.bfloat16), 'fsdp', scatter_dimensio...  40.5 us
    reduce_scatter x1, waiting for transfers between devices, body(): lax.psum_scatter(grad_down.astype(jnp.bfloat16), 'fsdp', scatter_dimensio...  40.4 us
    reduce_scatter x1, waiting for transfers between devices, body(): lax.psum_scatter(grad_up.astype(jnp.bfloat16), 'fsdp', scatter_dimension=...  40.4 us
    all_gather x1, waiting for transfers between devices, body(): lax.all_gather(w_up, 'fsdp', axis=0, tiled=True)  36.4 us
    all_gather x1, waiting for transfers between devices, body(): lax.all_gather(w_down, 'fsdp', axis=0, tiled=True)  35.2 us
    psum x1, blocking collectives, body(): lax.psum(shards[7].astype(jnp.bfloat16), ('rep', 'seq')).astype(jnp.float32)  34.6 us
    dot_general x9, matrix products, transpose_times(): lax.dot_general(left_side, right_side, (((0,), (0,)), ((), ())), preferre...  29.4 us
  transfers between devices with their start and end apart: 15, of which 12 were waited for; matrix products, arithmetic and copies ran while one was open for 13% of the time, Pallas kernels for 0%

commit v1 on v0

--- a/solution.py
+++ b/solution.py
@@ -271,7 +271,9 @@
         ).astype(jnp.float32),
     )
     totals = (
-        lax.psum(shards[0].astype(jnp.bfloat16), ("rep", "seq")).astype(jnp.float32),
+        jnp.sum(lax.all_gather(shards[0].astype(jnp.bfloat16), ("rep", "seq")), axis=0).astype(
+            jnp.float32
+        ),
         lax.psum(shards[1].astype(jnp.bfloat16), ("rep", "seq")).astype(jnp.float32),
         lax.psum(shards[2].astype(jnp.bfloat16), ("rep", "seq")).astype(jnp.float32),
         lax.psum(shards[3].astype(jnp.bfloat16), ("rep", "seq")).astype(jnp.float32),

time: 612 us -> 691 us (1.13)
  waiting for transfers between devices: 392 us -> 458 us
  other arithmetic: 28 us -> 35.1 us
    all_gather x0 -> x1, waiting for transfers between devices: none -> 78.8 us  [body(): lax.all_gather(shards[0].astype(jnp.bfloat16), ('rep', 'seq'))]
    psum x1, waiting for transfers between devices: 88.2 us -> 76.4 us  [body(): lax.psum(shards[1].astype(jnp.bfloat16), ('rep', 'seq')).astype(jnp.float32)]
  transfers between devices with their start and end apart: 15 -> 16, of which waited for: 12 -> 13; matrix products, arithmetic and copies ran while one was open for 13% -> 13% of each run, Pallas kernels for 0% -> 0%
where the time goes in v1:
time: 691 us; the launch traced here: 687 us
  waiting for transfers between devices  458 us (66%)
  blocking collectives  85.4 us (12%)
  matrix products  71.2 us (10%)
  other arithmetic  35.1 us (5%)
  local copies, waits for them, and re-layouts  18.6 us (3%)
  between operations  17.3 us (3%)
    all_gather x1, waiting for transfers between devices, body(): lax.all_gather(shards[0].astype(jnp.bfloat16), ('rep', 'seq'))  78.8 us
    psum x1, waiting for transfers between devices, body(): lax.psum(shards[1].astype(jnp.bfloat16), ('rep', 'seq')).astype(jnp.float32)  76.4 us
    reduce_scatter x1, waiting for transfers between devices, body(): lax.psum_scatter(grad_up.astype(jnp.bfloat16), 'fsdp', scatter_dimension=...  40.5 us
    reduce_scatter x1, waiting for transfers between devices, body(): lax.psum_scatter(grad_down.astype(jnp.bfloat16), 'fsdp', scatter_dimensio...  40.5 us
    reduce_scatter x1, waiting for transfers between devices, body(): lax.psum_scatter(grad_gate.astype(jnp.bfloat16), 'fsdp', scatter_dimensio...  40.4 us
    all_gather x1, waiting for transfers between devices, body(): lax.all_gather(w_up, 'fsdp', axis=0, tiled=True)  36.4 us
    all_gather x1, waiting for transfers between devices, body(): lax.all_gather(w_down, 'fsdp', axis=0, tiled=True)  35.2 us
    psum x1, blocking collectives, body(): lax.psum(shards[7].astype(jnp.bfloat16), ('rep', 'seq')).astype(jnp.float32)  34.3 us
  transfers between devices with their start and end apart: 16, of which 13 were waited for; matrix products, arithmetic and copies ran while one was open for 13% of the time, Pallas kernels for 0%

profile of v1, /device:TPU:0, one launch (start us, length us, event | category | flops | bytes accessed | tf_op | source)
XLA Modules:
  0.0 686.9 jit_solution(4013533533081355777)
XLA Ops:
  11.2 5.2 all-gather.1
  22.8 5.3 all-reduce.17
  29.0 10.0 %all_gather.61 = bf16[640,256]{1,0:T(8,128)(2,1)S(1)} all-gather(bf16[320,256]{1,0:T(8,128)(2,1)S(1)} %copy-done.38), channel_id=1, replica_groups=mesh['rep'=4,'fsdp'=2,'seq'=4] {'fsdp'}, dimensions={0}, use_global_device_ids=true | all-gather | bytes 491520 | tf_op jit(solution)/shard_map/all_gather | solution.py:86
  39.5 6.0 all_gather.64
  45.8 8.1 %all_gather.65 = bf16[1024,256]{1,0:T(8,128)(2,1)} all-gather(bf16[256,256]{1,0:T(8,128)(2,1)S(1)} %convolution_convert_fusion.10), channel_id=1, replica_groups=mesh['rep'=4,'fsdp'=2,'seq'=4] {'seq'}, dimensions={0}, use_global_device_ids=true | all-gather | bytes 655360 | tf_op jit(solution)/shard_map/all_gather | solution.py:137
  54.7 7.3 %all_gather.63 = bf16[1024,256]{0,1:T(8,128)(2,1)S(1)} all-gather(bf16[256,256]{0,1:T(8,128)(2,1)S(1)} %pad_maximum_fusion.3), channel_id=1, replica_groups=mesh['rep'=4,'fsdp'=2,'seq'=4] {'seq'}, dimensions={0}, use_global_device_ids=true | all-gather | bytes 655360 | tf_op jit(solution)/shard_map/all_gather | solution.py:136
  81.1 25.8 %all-gather.14.cloned.1.call-done = bf16[640,2048]{1,0:T(8,128)(2,1)} async-done(((bf16[320,2048]{1,0:T(8,128)(2,1)}), bf16[640,2048]{1,0:T(8,128)(2,1)}) %all-gather.14.cloned.1.call-update) | async-done | bytes 2621456 | tf_op jit(solution)/shard_map/all_gather | solution.py:89
  110.9 36.4 %all-gather.16.cloned.1.call-done = bf16[640,2048]{1,0:T(8,128)(2,1)} async-done(((bf16[320,2048]{1,0:T(8,128)(2,1)}), bf16[640,2048]{1,0:T(8,128)(2,1)}) %all-gather.16.cloned.1.call-update) | async-done | bytes 2621456 | tf_op jit(solution)/shard_map/all_gather | solution.py:90
  147.3 5.2 multiply_convert_fusion.2
  152.5 35.2 %all-gather.18.cloned.1.call-done = bf16[2048,640]{1,0:T(8,128)(2,1)} async-done(((bf16[1024,640]{1,0:T(8,128)(2,1)}), bf16[2048,640]{1,0:T(8,128)(2,1)}) %all-gather.18.cloned.1.call-update) | async-done | bytes 2621456 | tf_op jit(solution)/shard_map/all_gather | solution.py:91
  210.1 12.4 %fusion.27 = bf16[1024,256]{0,1:T(8,128)(2,1)} fusion(f32[256,4,1024]{2,0,1:T(8,128)} %fusion.54, f32[256,4,1024]{2,0,1:T(8,128)} %copy-done, f32[256,4]{0,1:T(4,128)S(1)} %log_add_fusion, bf16[256,4,128]{0,2,1:T(8,128)(2,1)} %copy-done.36, bf16[256,4,128]{0,2,1:T(8,128)(2,1)S(1)} %copy-done.35), kind=kOutput, calls=%fused_computation.34 | convolution fusion | flops 545523712 | bytes 9441280 | tf_op jit(solution)/shard_map/dot_general | solution.py:57
  222.6 6.5 reduce-scatter.12.cloned.1.call-done
  231.2 22.6 %reduce-scatter.10.cloned.1.call-done = bf16[256,256]{0,1:T(8,128)(2,1)} async-done(((bf16[1024,256]{0,1:T(8,128)(2,1)}), bf16[256,256]{0,1:T(8,128)(2,1)}) %reduce-scatter.10.cloned.1.call-update) | async-done | bytes 131088 | tf_op jit(solution)/shard_map/reduce_scatter | solution.py:210
  270.6 10.1 %fusion.9 = f32[256,4,256]{0,2,1:T(8,128)S(1)} fusion(f32[256,4,1024]{2,0,1:T(8,128)} %fusion.54, f32[256,4,1024]{2,0,1:T(8,128)} %copy-done, f32[256,4]{0,1:T(4,128)S(1)} %log_add_fusion, bf16[1024,256]{0,1:T(8,128)(2,1)S(1)} %copy-done.33), kind=kOutput, calls=%fused_computation.15 | convolution fusion | flops 544212992 | bytes 9965568 | tf_op jit(solution)/shard_map/dot_general | solution.py:47
  284.0 26.0 %reduce-scatter.20.cloned.1.call-done = bf16[512,640]{1,0:T(8,128)(2,1)} async-done(((bf16[1024,640]{1,0:T(8,128)(2,1)}), bf16[512,640]{1,0:T(8,128)(2,1)}) %reduce-scatter.20.cloned.1.call-update) | async-done | bytes 655376 | tf_op jit(solution)/shard_map/reduce_scatter | solution.py:242
  310.0 40.5 %reduce-scatter.24.cloned.1.call-done = bf16[320,2048]{1,0:T(8,128)(2,1)} async-done(((bf16[640,2048]{1,0:T(8,128)(2,1)}), bf16[320,2048]{1,0:T(8,128)(2,1)}) %reduce-scatter.24.cloned.1.call-update) | async-done | bytes 1310736 | tf_op jit(solution)/shard_map/reduce_scatter | solution.py:248
  350.5 40.4 %reduce-scatter.22.cloned.1.call-done = bf16[320,2048]{1,0:T(8,128)(2,1)} async-done(((bf16[640,2048]{1,0:T(8,128)(2,1)}), bf16[320,2048]{1,0:T(8,128)(2,1)}) %reduce-scatter.22.cloned.1.call-update) | async-done | bytes 1310736 | tf_op jit(solution)/shard_map/reduce_scatter | solution.py:245
  390.9 40.5 %reduce-scatter.26.cloned.1.call-done = bf16[1024,640]{1,0:T(8,128)(2,1)} async-done(((bf16[2048,640]{1,0:T(8,128)(2,1)}), bf16[1024,640]{1,0:T(8,128)(2,1)}) %reduce-scatter.26.cloned.1.call-update) | async-done | bytes 1310736 | tf_op jit(solution)/shard_map/reduce_scatter | solution.py:251
  431.5 25.9 %reduce-scatter.14.cloned.1.call-done = bf16[320,1024]{1,0:T(8,128)(2,1)} async-done(((bf16[640,1024]{1,0:T(8,128)(2,1)}), bf16[320,1024]{1,0:T(8,128)(2,1)}) %reduce-scatter.14.cloned.1.call-update) | async-done | bytes 655376 | tf_op jit(solution)/shard_map/reduce_scatter | solution.py:233
  461.0 5.1 all-reduce.16
  466.5 34.3 %all-reduce.14 = (bf16[320]{0:T(512)(128)(2,1)S(1)}, bf16[128]{0:T(256)(128)(2,1)S(1)}, bf16[128]{0:T(256)(128)(2,1)S(1)}, bf16[320]{0:T(512)(128)(2,1)S(1)}, bf...) all-reduce(bf16[320]{0:T(512)(128)(2,1)S(1)} %dynamic-slice.5, ...), channel_id=1, replica_groups=mesh['rep'=4,'fsdp'=2,'seq'=4] {'rep','seq'}, use_global_device_ids=true, to_apply=%region_36.37 | all-reduce | flops 1536 | bytes 6144 | tf_op jit(solution)/shard_map/psum | solution.py:283
  506.2 76.4 %all-reduce.20.cloned.1.call-done = (bf16[320,256]{1,0:T(8,128)(2,1)}, bf16[320,256]{1,0:T(8,128)(2,1)}, bf16[512,640]{1,0:T(8,128)(2,1)}, bf16[320,2048]{1,0:T(...) async-done(((bf16[320,256]{1,0:T(8,128)(2,1)}, bf16[320,256]{1,0:T(8,128)(2,1)}, bf16[512,640]{1,0:T(8,128)(2,1)}, bf16[320,2048]{1,0:T(8,128)(2,1)}, ...) | async-done | bytes 4915216 | tf_op jit(solution)/shard_map/psum | solution.py:277
  593.5 78.8 %all-gather.20.cloned.1.call-done = bf16[5120,1024]{1,0:T(8,128)(2,1)} async-done(((bf16[320,1024]{1,0:T(8,128)(2,1)}), bf16[5120,1024]{1,0:T(8,128)(2,1)}) %all-gather.20.cloned.1.call-update) | async-done | bytes 10485776 | tf_op jit(solution)/shard_map/all_gather | solution.py:274
  672.3 6.7 reduce_sum.233
  (315 shorter events, 99.2 us)
Async XLA Ops:
  7.2 55.9 %all-gather.10.cloned.1.call-start = ((), (), s32[]{:S(2)}) async-start(), calls=%async_computation.9 | async-start | bytes 1966080 | tf_op jit(solution)/shard_map/all_gather | solution.py:85
  7.9 69.5 %all-gather.12.cloned.1.call-start = ((), (), s32[]{:S(2)}) async-start(), calls=%async_computation.10 | async-start | bytes 1966080 | tf_op jit(solution)/shard_map/all_gather | solution.py:88
  8.8 98.1 %all-gather.14.cloned.1.call-start = ((), (), s32[]{:S(2)}) async-start(), calls=%async_computation.11 | async-start | bytes 3932160 | tf_op jit(solution)/shard_map/all_gather | solution.py:89
  9.5 137.8 %all-gather.16.cloned.1.call-start = ((), (), s32[]{:S(2)}) async-start(), calls=%async_computation.12 | async-start | bytes 3932160 | tf_op jit(solution)/shard_map/all_gather | solution.py:90
  10.1 177.6 %all-gather.18.cloned.1.call-start = ((), (), s32[]{:S(2)}) async-start(), calls=%async_computation.13 | async-start | bytes 3932160 | tf_op jit(solution)/shard_map/all_gather | solution.py:91
  10.7 218.4 %reduce-scatter.12.cloned.1.call-start = ((), (), s32[]{:S(2)}) async-start(), calls=%async_computation.15 | async-start | bytes 655360 | tf_op jit(solution)/shard_map/reduce_scatter | solution.py:213
  10.8 43.3 %copy-start.74 = (f32[128]{0:T(128)}, f32[128]{0:T(128)S(1)}, u32[]{:S(2)}) copy-start(f32[128]{0:T(128)S(1)} %multiply_power_fusion) | copy-start | bytes 1540
  11.1 42.9 %copy-start.62 = (f32[256]{0:T(256)}, f32[256]{0:T(256)S(1)}, u32[]{:S(2)}) copy-start(f32[256]{0:T(256)S(1)} %fusion.45) | copy-start | bytes 3076
  11.1 54.1 %copy-start.48 = (f32[256]{0:T(256)}, f32[256]{0:T(256)S(1)}, u32[]{:S(2)}) copy-start(f32[256]{0:T(256)S(1)} %fusion.83) | copy-start | bytes 3076
  16.3 49.7 %copy-start.52 = (f32[2,1,128]{2,1,0:T(1,128)}, f32[2,1,128]{2,1,0:T(1,128)S(1)}, u32[]{:S(2)}) copy-start(f32[2,1,128]{2,1,0:T(1,128)S(1)} %convert_element_type.286) | copy-start | bytes 3076
  20.6 33.5 %copy-start.54 = (f32[2,1,128]{2,1,0:T(1,128)}, f32[2,1,128]{2,1,0:T(1,128)S(1)}, u32[]{:S(2)}) copy-start(f32[2,1,128]{2,1,0:T(1,128)S(1)} %convert_element_type.287) | copy-start | bytes 3076
  207.2 46.6 %reduce-scatter.10.cloned.1.call-start = ((), (), s32[]{:S(2)}) async-start(), calls=%async_computation.14 | async-start | bytes 655360 | tf_op jit(solution)/shard_map/reduce_scatter | solution.py:210
  222.5 33.0 %copy-start.72 = (f32[256]{0:T(256)S(1)}, f32[256]{0:T(256)}, u32[]{:S(2)}) copy-start(f32[256]{0:T(256)} %copy-done.71) | copy-start | bytes 3076
  222.6 61.3 %reduce-scatter.18.cloned.1.call-start = ((), (), s32[]{:S(2)}) async-start(), calls=%async_computation.18 | async-start | bytes 491520 | tf_op jit(solution)/shard_map/reduce_scatter | solution.py:239
  231.2 52.8 %reduce-scatter.16.cloned.1.call-start = ((), (), s32[]{:S(2)}) async-start(), calls=%async_computation.17 | async-start | bytes 491520 | tf_op jit(solution)/shard_map/reduce_scatter | solution.py:236
  256.8 53.1 %reduce-scatter.20.cloned.1.call-start = ((), (), s32[]{:S(2)}) async-start(), calls=%async_computation.19 | async-start | bytes 1966080 | tf_op jit(solution)/shard_map/reduce_scatter | solution.py:242
  259.6 90.9 %reduce-scatter.24.cloned.1.call-start = ((), (), s32[]{:S(2)}) async-start(), calls=%async_computation.21 | async-start | bytes 3932160 | tf_op jit(solution)/shard_map/reduce_scatter | solution.py:248
  262.1 128.8 %reduce-scatter.22.cloned.1.call-start = ((), (), s32[]{:S(2)}) async-start(), calls=%async_computation.20 | async-start | bytes 3932160 | tf_op jit(solution)/shard_map/reduce_scatter | solution.py:245
  265.7 165.7 %reduce-scatter.26.cloned.1.call-start = ((), (), s32[]{:S(2)}) async-start(), calls=%async_computation.22 | async-start | bytes 3932160 | tf_op jit(solution)/shard_map/reduce_scatter | solution.py:251
  269.6 187.8 %reduce-scatter.14.cloned.1.call-start = ((), (), s32[]{:S(2)}) async-start(), calls=%async_computation.16 | async-start | bytes 1966080 | tf_op jit(solution)/shard_map/reduce_scatter | solution.py:233
  283.8 298.8 %all-reduce.20.cloned.1.call-start = ((), (), s32[]{:S(2)}) async-start(), calls=%async_computation.24 | async-start | bytes 9830400 | tf_op jit(solution)/shard_map/psum | solution.py:277
  431.4 240.9 %all-gather.20.cloned.1.call-start = ((), (), s32[]{:S(2)}) async-start(), calls=%async_computation.23 | async-start | bytes 11141120 | tf_op jit(solution)/shard_map/all_gather | solution.py:274
  459.4 44.7 %copy-start.63 = (f32[256]{0:T(256)S(1)}, f32[256]{0:T(256)}, u32[]{:S(2)}) copy-start(f32[256]{0:T(256)} %copy-done.62) | copy-start | bytes 3076
  459.4 44.8 %copy-start.3 = (f32[256,640]{1,0:T(8,128)S(1)}, f32[256,640]{1,0:T(8,128)}, u32[]{:S(2)}) copy-start(f32[256,640]{1,0:T(8,128)} %copy-done.2) | copy-start | bytes 1966084
  (77 other events, 680.3 us)
Sparse Core Ops, SparseCore 0:
  9.5 31.1 all-gather.9
  42.2 24.0 all-gather.11
  67.8 38.9 all-gather.13
  108.3 38.9 all-gather.15
  148.7 38.9 all-gather.17
  207.4 21.6 reduce-scatter.11
  232.1 21.6 reduce-scatter.9
  256.1 12.4 reduce-scatter.17
  271.4 12.5 reduce-scatter.15
  286.7 23.2 reduce-scatter.19
  312.8 37.6 reduce-scatter.23
  353.2 37.6 reduce-scatter.21
  393.7 37.6 reduce-scatter.25
  434.1 23.2 reduce-scatter.13
  461.7 120.8 all-reduce.19
  584.7 87.5 all-gather.19
